TPU v7x, 32 devices: a whole 2x2x4 slice. The times are simulated.
32 devices in a mesh: dp: 8 (over z, y), inner: 4 (over x, core).
Axes of the slice: x: 2, y: 2, z: 4, core: 2. Of those that a mesh axis runs over, the one named last changes fastest.
Arguments:
- tokens: bfloat16 [32768, 512], P(('dp', 'inner')), may hold values from -6 to 6
- segments: int32 [32768], P(('dp', 'inner')), may hold values from 0 to 32767, as said below
- positions: int32 [32768], P(('dp', 'inner')), may hold values from 0 to 1023, as said below
- cotangent: bfloat16 [32768, 512], P(('dp', 'inner')), may hold values from -6 to 6
- attn_weight: float32 [4, 512, 512], P(None, ('dp', 'inner')), may hold values from -0.53033009 to 0.53033009
- attn_m: float32 [4, 512, 512], P(None, ('dp', 'inner')), may hold values from -0.0007324219 to 0.0007324219
- attn_v: float32 [4, 512, 512], P(None, ('dp', 'inner')), may hold values from 1.0882435e-09 to 4.352974e-09
- gate_weight: float32 [2, 512, 512], P(None, ('dp', 'inner')), may hold values from -0.25 to 0.25
- gate_m: float32 [2, 512, 512], P(None, ('dp', 'inner')), may hold values from -0.00036621094 to 0.00036621094
- gate_v: float32 [2, 512, 512], P(None, ('dp', 'inner')), may hold values from 2.7206087e-10 to 1.0882435e-09
- in_weight: float32 [512, 2048], P(('dp', 'inner')), may hold values from -0.25 to 0.25
- in_m: float32 [512, 2048], P(('dp', 'inner')), may hold values from -0.00036621094 to 0.00036621094
- in_v: float32 [512, 2048], P(('dp', 'inner')), may hold values from 2.7206087e-10 to 1.0882435e-09
- out_weight: float32 [2048, 512], P(('dp', 'inner')), may hold values from -0.125 to 0.125
- out_m: float32 [2048, 512], P(('dp', 'inner')), may hold values from -0.00036621094 to 0.00036621094
- out_v: float32 [2048, 512], P(('dp', 'inner')), may hold values from 2.7206087e-10 to 1.0882435e-09
- norm_params: float32 [7, 512], P(None, ('dp', 'inner'))
- norm_m: float32 [7, 512], P(None, ('dp', 'inner')), may hold values from -0.0014648438 to 0.0014648438
- norm_v: float32 [7, 512], P(None, ('dp', 'inner')), may hold values from 4.352974e-09 to 1.7411896e-08
- in_bias: float32 [2048], P(('dp', 'inner')), may hold values from -1.75 to 1.75
- bias_m: float32 [2048], P(('dp', 'inner')), may hold values from -0.00024414062 to 0.00024414062
- bias_v: float32 [2048], P(('dp', 'inner')), may hold values from 1.7411896e-10 to 7.073583e-10
Outputs:
- layer_out: bfloat16 [32768, 512], P(('dp', 'inner'))
- input_grad: bfloat16 [32768, 512], P(('dp', 'inner'))
- grad_norm: float32 [], replicated
- attn_new: float32 [4, 512, 512], P(None, ('dp', 'inner'))
- attn_m_new: float32 [4, 512, 512], P(None, ('dp', 'inner'))
- attn_v_new: float32 [4, 512, 512], P(None, ('dp', 'inner'))
- gate_new: float32 [2, 512, 512], P(None, ('dp', 'inner'))
- gate_m_new: float32 [2, 512, 512], P(None, ('dp', 'inner'))
- gate_v_new: float32 [2, 512, 512], P(None, ('dp', 'inner'))
- in_new: float32 [512, 2048], P(('dp', 'inner'))
- in_m_new: float32 [512, 2048], P(('dp', 'inner'))
- in_v_new: float32 [512, 2048], P(('dp', 'inner'))
- out_new: float32 [2048, 512], P(('dp', 'inner'))
- out_m_new: float32 [2048, 512], P(('dp', 'inner'))
- out_v_new: float32 [2048, 512], P(('dp', 'inner'))
- norm_new: float32 [7, 512], P(None, ('dp', 'inner'))
- norm_m_new: float32 [7, 512], P(None, ('dp', 'inner'))
- norm_v_new: float32 [7, 512], P(None, ('dp', 'inner'))
- bias_new: float32 [2048], P(('dp', 'inner'))
- bias_m_new: float32 [2048], P(('dp', 'inner'))
- bias_v_new: float32 [2048], P(('dp', 'inner'))
Inputs may be any that keep to these rules, and one draw needn't show every extreme that they name: `segments`: a token's segment number is the index of its document's first token, so segment numbers never fall; a new document begins at every sequence start (every 1024 tokens); the first sequence is one document; the last token forms a document of its own. positions restart at 0 with every new segment number.
All inputs are finite; a program needn't handle non-finite values.
Results may differ from a plain program's by a relative error of at most 0.033.
The roundings to bfloat16 on the way count: a program that leaves them out, or rounds other values in their place, can miss the bound.
Values may be sent and summed in bfloat16 or wider, within the bound.
No kernel may reach another device: no remote copies, remote signals or barrier semaphores. Data moves between devices by JAX's collectives and lax.ppermute only.
A program may use at most 192 MiB of HBM per device.

v0:
```python
import jax
import jax.numpy as jnp
from jax import lax
from jax.sharding import PartitionSpec as P

HEADS = 8
HEAD = 64
STEP = 10
norm_eps = 1e-05
first_decay = 0.9
second_decay = 0.999
adam_eps = 1e-08
learn_rate = 0.05
vector_rate = 0.8
weight_decay = 0.1
clip_norm = 1.0
masked_score = -1e30


def normalize_parts(values, gain_row, bias_row):
    centred = values - jnp.mean(values, -1, keepdims=True)
    spread = jnp.mean(centred * centred, -1, keepdims=True)
    scale_row = lax.rsqrt(spread + norm_eps)
    unit_rows = centred * scale_row
    return (unit_rows * gain_row + bias_row, unit_rows, scale_row)


def normalize_back(grad_rows, unit_rows, scale_row, gain_row):
    grad_unit = grad_rows * gain_row
    return scale_row * (
        grad_unit
        - jnp.mean(grad_unit, -1, keepdims=True)
        - unit_rows * jnp.mean(grad_unit * unit_rows, -1, keepdims=True)
    )


def fetch(shards):
    low_attn, low_gate, low_in, low_out, low_vec, low_shift = [
        element.astype(jnp.bfloat16) for element in shards
    ]
    return (
        lax.all_gather(low_attn, ("dp", "inner"), axis=1, tiled=True),
        lax.all_gather(low_gate, ("dp", "inner"), axis=1, tiled=True),
        lax.all_gather(low_in, ("dp", "inner"), axis=0, tiled=True),
        lax.all_gather(low_out, ("dp", "inner"), axis=0, tiled=True),
        lax.all_gather(low_vec, ("dp", "inner"), axis=1, tiled=True),
        lax.all_gather(low_shift, ("dp", "inner"), axis=0, tiled=True),
    )


def score_block(queries, key_heads, segments, positions, first_row, block_size):
    query_part = lax.slice_in_dim(queries, first_row, first_row + block_size, axis=0)
    raw_scores = jnp.einsum(
        "qhe,khe->hqk", query_part, key_heads, preferred_element_type=jnp.float32
    )
    own_segments = lax.slice_in_dim(segments, first_row, first_row + block_size, axis=0)
    own_positions = lax.slice_in_dim(positions, first_row, first_row + block_size, axis=0)
    allowed = (own_segments[:, None] == segments[None, :]) & (
        positions[None, :] <= own_positions[:, None]
    )
    return (jnp.where(allowed[None], raw_scores * HEAD ** (-0.5), masked_score), query_part)


def attend(triple, segments, positions):
    row_count = triple.shape[1]
    block_size = min(512, row_count)
    queries = triple[0].reshape(row_count, HEADS, HEAD)
    key_heads = triple[1].reshape(row_count, HEADS, HEAD)
    value_heads = triple[2].reshape(row_count, HEADS, HEAD)
    mixed_parts = []
    total_parts = []
    for first_row in range(0, row_count, block_size):
        scores, query_part = score_block(
            queries, key_heads, segments, positions, first_row, block_size
        )
        row_max = jnp.max(scores, -1, keepdims=True)
        weights = jnp.exp(scores - row_max)
        exp_total = jnp.sum(weights, -1, keepdims=True)
        attn_probs = (weights / exp_total).astype(jnp.bfloat16)
        mixed_block = jnp.einsum(
            "hqk,khe->qhe", attn_probs, value_heads, preferred_element_type=jnp.float32
        )
        mixed_parts.append(mixed_block.reshape(block_size, HEADS * HEAD))
        total_parts.append(row_max + jnp.log(exp_total))
    mixed_heads = jnp.concatenate(mixed_parts, 0).astype(jnp.bfloat16)
    return (mixed_heads, jnp.concatenate(total_parts, 1))


def attend_back(triple, grad_mixed, log_total, segments, positions):
    row_count = triple.shape[1]
    block_size = min(512, row_count)
    queries = triple[0].reshape(row_count, HEADS, HEAD)
    key_heads = triple[1].reshape(row_count, HEADS, HEAD)
    value_heads = triple[2].reshape(row_count, HEADS, HEAD)
    grad_heads = grad_mixed.reshape(row_count, HEADS, HEAD)
    query_grads = []
    grad_keys = jnp.zeros((row_count, HEADS, HEAD), jnp.float32)
    grad_values = jnp.zeros((row_count, HEADS, HEAD), jnp.float32)
    for first_row in range(0, row_count, block_size):
        scores, query_part = score_block(
            queries, key_heads, segments, positions, first_row, block_size
        )
        attn_probs = jnp.exp(
            scores - lax.slice_in_dim(log_total, first_row, first_row + block_size, axis=1)
        )
        grad_part = lax.slice_in_dim(grad_heads, first_row, first_row + block_size, axis=0)
        grad_probs = jnp.einsum(
            "qhe,khe->hqk", grad_part, value_heads, preferred_element_type=jnp.float32
        )
        row_inner = jnp.sum(attn_probs * grad_probs, -1, keepdims=True)
        grad_raw = (attn_probs * (grad_probs - row_inner) * HEAD ** (-0.5)).astype(jnp.bfloat16)
        query_grads.append(
            jnp.einsum(
                "hqk,khe->qhe", grad_raw, key_heads, preferred_element_type=jnp.float32
            ).reshape(block_size, HEADS * HEAD)
        )
        grad_keys = grad_keys + jnp.einsum(
            "hqk,qhe->khe", grad_raw, query_part, preferred_element_type=jnp.float32
        )
        grad_values = grad_values + jnp.einsum(
            "hqk,qhe->khe",
            attn_probs.astype(jnp.bfloat16),
            grad_part,
            preferred_element_type=jnp.float32,
        )
    grad_query_rows = jnp.concatenate(query_grads, 0)
    stacked = jnp.stack(
        [
            grad_query_rows,
            grad_keys.reshape(row_count, HEADS * HEAD),
            grad_values.reshape(row_count, HEADS * HEAD),
        ]
    )
    return stacked.astype(jnp.bfloat16)


def attn_branch(weights, normed, segments, positions):
    triple = jnp.einsum(
        "td,jde->jte", normed, weights[0][:3], preferred_element_type=jnp.float32
    ).astype(jnp.bfloat16)
    mixed_heads, log_total = attend(triple, segments, positions)
    attended = jnp.dot(mixed_heads, weights[0][3], preferred_element_type=jnp.float32)
    return (triple, mixed_heads, log_total, attended)


def ffn_branch(weights, normed_two):
    hidden = jnp.dot(normed_two, weights[2], preferred_element_type=jnp.float32) + weights[
        5
    ].astype(jnp.float32)
    active = jnp.maximum(hidden, 0.0).astype(jnp.bfloat16)
    branch = jnp.dot(active, weights[3], preferred_element_type=jnp.float32) + weights[4][6].astype(
        jnp.float32
    )
    return (hidden, active, branch)


def adam_update(weight, first_moment, second_moment, gradient, factor, step_rate):
    clipped = gradient * factor
    first_new = first_decay * first_moment + (1.0 - first_decay) * clipped
    second_new = second_decay * second_moment + (1.0 - second_decay) * clipped * clipped
    corrected = first_new / (1.0 - first_decay**STEP)
    spread = second_new / (1.0 - second_decay**STEP)
    weight_new = weight - step_rate * (
        corrected / (jnp.sqrt(spread) + adam_eps) + weight_decay * weight
    )
    return (weight_new, first_new, second_new)


def body(
    tokens,
    segments,
    positions,
    cotangent,
    attn_weight,
    attn_m,
    attn_v,
    gate_weight,
    gate_m,
    gate_v,
    in_weight,
    in_m,
    in_v,
    out_weight,
    out_m,
    out_v,
    norm_params,
    norm_m,
    norm_v,
    in_bias,
    bias_m,
    bias_v,
):
    shards = (attn_weight, gate_weight, in_weight, out_weight, norm_params, in_bias)
    weights = fetch(shards)
    vectors = weights[4].astype(jnp.float32)
    inputs = tokens.astype(jnp.float32)
    normed_full, unit_one, scale_one = normalize_parts(inputs, vectors[0], vectors[1])
    normed = normed_full.astype(jnp.bfloat16)
    triple, mixed_heads, log_total, attended = attn_branch(weights, normed, segments, positions)
    attn_gate = jax.nn.sigmoid(
        jnp.dot(normed, weights[1][0], preferred_element_type=jnp.float32) + vectors[4]
    )
    middle = attn_gate * attended + (1.0 - attn_gate) * inputs
    normed_two_full, unit_two, scale_two = normalize_parts(middle, vectors[2], vectors[3])
    normed_two = normed_two_full.astype(jnp.bfloat16)
    hidden, active, branch = ffn_branch(weights, normed_two)
    ffn_gate = jax.nn.sigmoid(
        jnp.dot(normed_two, weights[1][1], preferred_element_type=jnp.float32) + vectors[5]
    )
    layer_out = (ffn_gate * branch + (1.0 - ffn_gate) * middle).astype(jnp.bfloat16)
    weights = fetch(shards)
    triple, mixed_heads, log_total, attended = attn_branch(weights, normed, segments, positions)
    hidden, active, branch = ffn_branch(weights, normed_two)
    grad_out = cotangent.astype(jnp.float32)
    grad_branch = grad_out * ffn_gate
    grad_fgate = grad_out * (branch - middle) * ffn_gate * (1.0 - ffn_gate)
    grad_middle = grad_out * (1.0 - ffn_gate)
    branch_low = grad_branch.astype(jnp.bfloat16)
    grad_w_out = jnp.einsum("tf,td->fd", active, branch_low, preferred_element_type=jnp.float32)
    grad_active = jnp.einsum(
        "td,fd->tf", branch_low, weights[3], preferred_element_type=jnp.float32
    )
    grad_hidden = jnp.where(hidden > 0.0, grad_active, 0.0)
    hidden_low = grad_hidden.astype(jnp.bfloat16)
    grad_w_in = jnp.einsum("td,tf->df", normed_two, hidden_low, preferred_element_type=jnp.float32)
    fgate_low = grad_fgate.astype(jnp.bfloat16)
    grad_w_fgate = jnp.einsum(
        "td,te->de", normed_two, fgate_low, preferred_element_type=jnp.float32
    )
    grad_normed_two = jnp.einsum(
        "tf,df->td", hidden_low, weights[2], preferred_element_type=jnp.float32
    )
    grad_normed_two = grad_normed_two + jnp.einsum(
        "te,de->td", fgate_low, weights[1][1], preferred_element_type=jnp.float32
    )
    grad_gain_two = jnp.sum(grad_normed_two * unit_two, 0)
    grad_shift_two = jnp.sum(grad_normed_two, 0)
    grad_middle = grad_middle + normalize_back(grad_normed_two, unit_two, scale_two, vectors[2])
    grad_attended = grad_middle * attn_gate
    grad_agate = grad_middle * (attended - inputs) * attn_gate * (1.0 - attn_gate)
    grad_inputs = grad_middle * (1.0 - attn_gate)
    attended_low = grad_attended.astype(jnp.bfloat16)
    grad_w_o = jnp.einsum(
        "td,te->de", mixed_heads, attended_low, preferred_element_type=jnp.float32
    )
    grad_mixed = jnp.einsum(
        "te,de->td", attended_low, weights[0][3], preferred_element_type=jnp.float32
    ).astype(jnp.bfloat16)
    triple_grad = attend_back(triple, grad_mixed, log_total, segments, positions)
    grad_w_qkv = jnp.einsum("td,jte->jde", normed, triple_grad, preferred_element_type=jnp.float32)
    agate_low = grad_agate.astype(jnp.bfloat16)
    grad_w_agate = jnp.einsum("td,te->de", normed, agate_low, preferred_element_type=jnp.float32)
    grad_normed = jnp.einsum(
        "jte,jde->td", triple_grad, weights[0][:3], preferred_element_type=jnp.float32
    )
    grad_normed = grad_normed + jnp.einsum(
        "te,de->td", agate_low, weights[1][0], preferred_element_type=jnp.float32
    )
    grad_gain_one = jnp.sum(grad_normed * unit_one, 0)
    grad_shift_one = jnp.sum(grad_normed, 0)
    grad_inputs = grad_inputs + normalize_back(grad_normed, unit_one, scale_one, vectors[0])
    input_grad = grad_inputs.astype(jnp.bfloat16)
    grad_attn = jnp.concatenate([grad_w_qkv, grad_w_o[None]], 0)
    grad_gates = jnp.stack([grad_w_agate, grad_w_fgate])
    grad_vectors = jnp.stack(
        [
            grad_gain_one,
            grad_shift_one,
            grad_gain_two,
            grad_shift_two,
            jnp.sum(grad_agate, 0),
            jnp.sum(grad_fgate, 0),
            jnp.sum(grad_branch, 0),
        ]
    )
    grad_bias = jnp.sum(grad_hidden, 0)
    owned = (
        lax.psum_scatter(grad_attn, ("dp", "inner"), scatter_dimension=1, tiled=True),
        lax.psum_scatter(grad_gates, ("dp", "inner"), scatter_dimension=1, tiled=True),
        lax.psum_scatter(grad_w_in, ("dp", "inner"), scatter_dimension=0, tiled=True),
        lax.psum_scatter(grad_w_out, ("dp", "inner"), scatter_dimension=0, tiled=True),
        lax.psum_scatter(grad_vectors, ("dp", "inner"), scatter_dimension=1, tiled=True),
        lax.psum_scatter(grad_bias, ("dp", "inner"), scatter_dimension=0, tiled=True),
    )
    local_squares = sum((jnp.sum(element * element) for element in owned))
    grad_norm = jnp.sqrt(lax.psum(local_squares, ("dp", "inner")))
    factor = jnp.minimum(1.0, clip_norm / (grad_norm + 1e-06))
    states = (
        (attn_weight, attn_m, attn_v),
        (gate_weight, gate_m, gate_v),
        (in_weight, in_m, in_v),
        (out_weight, out_m, out_v),
        (norm_params, norm_m, norm_v),
        (in_bias, bias_m, bias_v),
    )
    step_rates = (learn_rate, learn_rate, learn_rate, learn_rate, vector_rate, vector_rate)
    updated = [
        adam_update(state[0], state[1], state[2], gradient, factor, step_rate)
        for state, gradient, step_rate in zip(states, owned, step_rates)
    ]
    return (
        layer_out,
        input_grad,
        grad_norm,
        updated[0][0],
        updated[0][1],
        updated[0][2],
        updated[1][0],
        updated[1][1],
        updated[1][2],
        updated[2][0],
        updated[2][1],
        updated[2][2],
        updated[3][0],
        updated[3][1],
        updated[3][2],
        updated[4][0],
        updated[4][1],
        updated[4][2],
        updated[5][0],
        updated[5][1],
        updated[5][2],
    )


def solution(mesh):
    return jax.shard_map(
        body,
        mesh=mesh,
        in_specs=(
            P(("dp", "inner"), None),
            P(("dp", "inner")),
            P(("dp", "inner")),
            P(("dp", "inner"), None),
            P(None, ("dp", "inner"), None),
            P(None, ("dp", "inner"), None),
            P(None, ("dp", "inner"), None),
            P(None, ("dp", "inner"), None),
            P(None, ("dp", "inner"), None),
            P(None, ("dp", "inner"), None),
            P(("dp", "inner"), None),
            P(("dp", "inner"), None),
            P(("dp", "inner"), None),
            P(("dp", "inner"), None),
            P(("dp", "inner"), None),
            P(("dp", "inner"), None),
            P(None, ("dp", "inner")),
            P(None, ("dp", "inner")),
            P(None, ("dp", "inner")),
            P(("dp", "inner")),
            P(("dp", "inner")),
            P(("dp", "inner")),
        ),
        out_specs=(
            P(("dp", "inner"), None),
            P(("dp", "inner"), None),
            P(),
            P(None, ("dp", "inner"), None),
            P(None, ("dp", "inner"), None),
            P(None, ("dp", "inner"), None),
            P(None, ("dp", "inner"), None),
            P(None, ("dp", "inner"), None),
            P(None, ("dp", "inner"), None),
            P(("dp", "inner"), None),
            P(("dp", "inner"), None),
            P(("dp", "inner"), None),
            P(("dp", "inner"), None),
            P(("dp", "inner"), None),
            P(("dp", "inner"), None),
            P(None, ("dp", "inner")),
            P(None, ("dp", "inner")),
            P(None, ("dp", "inner")),
            P(("dp", "inner")),
            P(("dp", "inner")),
            P(("dp", "inner")),
        ),
        check_vma=False,
    )
```

profile of v0, /device:TPU:12, one launch (start us, length us, event | category | flops | bytes accessed | tf_op | source)
XLA Modules:
  0.0 1210.4 jit_solution(3663491869928504730)
XLA Ops:
  17.4 41.7 %all-reduce = bf16[2048]{0:T(1024)(128)(2,1)S(1)} all-reduce(bf16[2048]{0:T(1024)(128)(2,1)S(1)} %dynamic-update-slice), channel_id=1, replica_groups=mesh['dp'=8,'inner'=4] {'dp','inner'}, use_global_device_ids=true, to_apply=%add | all-reduce | flops 2048 | bytes 8192
  59.1 29.3 %all-gather = bf16[32,16,7]{1,2,0:T(8,128)(2,1)S(1)} all-gather(bf16[1,16,7]{1,2,0:T(8,128)(2,1)S(1)} %convert_bitcast_fusion.1), channel_id=1, replica_groups=mesh['dp'=8,'inner'=4] {'dp','inner'}, dimensions={0}, use_global_device_ids=true | all-gather | bytes 7392 | tf_op jit(solution)/shard_map/all_gather | solution.py:46
  90.0 4.1 copy.135
  107.4 3.8 fusion.82
  114.5 4.1 fusion.8
  120.8 3.8 fusion.83
  127.5 5.1 fusion.131
  133.1 49.7 %all-gather.10.cloned.1.call-done = bf16[512,2048]{1,0:T(8,128)(2,1)} async-done(((bf16[16,2048]{1,0:T(8,128)(2,1)}), bf16[512,2048]{1,0:T(8,128)(2,1)}) %all-gather.10.cloned.1.call-update) | async-done | bytes 2097168 | tf_op jit(solution)/shard_map/all_gather | solution.py:44
  182.8 7.2 fusion.142
  190.0 51.2 %all-gather.12.cloned.1.call-done = bf16[2048,512]{1,0:T(8,128)(2,1)} async-done(((bf16[64,512]{1,0:T(8,128)(2,1)}), bf16[2048,512]{1,0:T(8,128)(2,1)}) %all-gather.12.cloned.1.call-update) | async-done | bytes 2097168 | tf_op jit(solution)/shard_map/all_gather | solution.py:45
  241.2 6.5 fusion.86
  267.3 8.1 fusion.143
  275.3 29.8 %fusion.79 = bf16[8,64,512]{2,1,0:T(8,128)(2,1)} fusion(bf16[1024,8,64]{0,2,1:T(8,128)(2,1)} %bitcast.126, f32[8,512,1024]{2,1,0:T(8,128)} %fusion.143, f32[8,512,1024]{2,1,0:T(8,128)} %copy-done.1, f32[8,512]{1,0:T(8,128)S(1)} %log_add_fusion.1), kind=kOutput, calls=%fused_computation.102 | convolution fusion | flops 566498304 | bytes 35143680 | tf_op jit(solution)/shard_map/hqk,khe->qhe/dot_general | solution.py:113
  305.1 31.1 %fusion.13 = f32[8,64,1024]{2,1,0:T(8,128)} fusion(bf16[512,8,64]{0,2,1:T(8,128)(2,1)} %bitcast.137, f32[8,512,1024]{2,1,0:T(8,128)} %fusion.143, f32[8,512,1024]{2,1,0:T(8,128)} %copy-done.1, f32[8,512]{1,0:T(8,128)S(1)} %log_add_fusion.1), kind=kOutput, calls=%fused_computation.20 | convolution fusion | flops 566236160 | bytes 36192256 | tf_op jit(solution)/shard_map/hqk,qhe->khe/dot_general | solution.py:117
  336.2 9.5 fusion.144
  345.8 7.4 fusion.24
  353.3 3.9 add_convert_fusion
  361.6 37.1 %fusion.76 = bf16[8,64,512]{2,1,0:T(8,128)(2,1)} fusion(bf16[1024,8,64]{0,2,1:T(8,128)(2,1)S(1)} %bitcast.127, f32[8,512,1024]{2,1,0:T(8,128)} %fusion.144, f32[8,512,1024]{2,1,0:T(8,128)} %copy-done, f32[8,512]{1,0:T(8,128)S(1)} %log_add_fusion), kind=kOutput, calls=%fused_computation.101 | convolution fusion | flops 566498304 | bytes 35143680 | tf_op jit(solution)/shard_map/hqk,khe->qhe/dot_general | solution.py:113
  398.7 31.8 %add_convert_fusion.1 = bf16[8,64,1024]{2,1,0:T(8,128)(2,1)} fusion(f32[8,64,1024]{2,1,0:T(8,128)} %fusion.13, bf16[512,8,64]{0,2,1:T(8,128)(2,1)} %bitcast.135, f32[8,512,1024]{2,1,0:T(8,128)} %fusion.144, f32[8,512,1024]{2,1,0:T(8,128)} %copy-done, f32[8,512]{1,0:T(8,128)S(1)} %log_add_fusion), kind=kOutput, calls=%fused_computation.76 | convolution fusion | flops 567284736 | bytes 37240832 | tf_op jit(solution)/shard_map/hqk,qhe->khe/dot_general | solution.py:117
  439.0 3.7 convolution_bitcast_fusion
  446.3 4.6 pad_maximum_fusion
  450.9 5.4 copy.128
  461.7 6.7 fusion.66
  470.0 8.0 fusion.85
  478.0 40.1 %all-reduce.2 = f32[2048]{0:T(1024)S(1)} all-reduce(f32[2048]{0:T(1024)S(1)} %get-tuple-element.168), channel_id=7, replica_groups=mesh['dp'=8,'inner'=4] {'dp','inner'}, use_global_device_ids=true, to_apply=%region_32.33.clone | all-reduce | flops 2048 | bytes 16384
  519.4 34.3 %reduce-scatter.13.cloned.1.call-done = f32[16,7]{1,0:T(8,128)} async-done(((f32[512,7]{1,0:T(8,128)}), f32[16,7]{1,0:T(8,128)}) %reduce-scatter.13.cloned.1.call-update) | async-done | bytes 464
  555.1 169.7 %all-reduce.5.cloned.1.call-done = f32[4,512,512]{2,0,1:T(4,128)} async-done(((f32[4,512,512]{2,0,1:T(4,128)}), f32[4,512,512]{2,0,1:T(4,128)}) %all-reduce.5.cloned.1.call-update) | async-done | bytes 4194320
  727.0 110.1 %reduce-scatter.7.cloned.1.call-done = f32[2,16,512]{2,1,0:T(8,128)} async-done(((f32[2,512,512]{2,1,0:T(8,128)}), f32[2,16,512]{2,1,0:T(8,128)}) %reduce-scatter.7.cloned.1.call-update) | async-done | bytes 65552 | tf_op jit(solution)/shard_map/reduce_scatter | solution.py:279
  839.9 137.9 %reduce-scatter.9.cloned.1.call-done = f32[16,2048]{1,0:T(8,128)} async-done(((f32[512,2048]{1,0:T(8,128)}), f32[16,2048]{1,0:T(8,128)}) %reduce-scatter.9.cloned.1.call-update) | async-done | bytes 131088 | tf_op jit(solution)/shard_map/reduce_scatter | solution.py:280
  979.9 138.4 %reduce-scatter.11.cloned.1.call-done = f32[64,512]{1,0:T(8,128)} async-done(((f32[2048,512]{1,0:T(8,128)}), f32[64,512]{1,0:T(8,128)}) %reduce-scatter.11.cloned.1.call-update) | async-done | bytes 131088 | tf_op jit(solution)/shard_map/reduce_scatter | solution.py:281
  1121.9 3.7 fusion.56
  1125.6 67.5 %psum.7 = f32[]{:T(128)} all-reduce(f32[]{:T(128)S(6)} %add.297), channel_id=1, replica_groups=mesh['dp'=8,'inner'=4] {'dp','inner'}, use_global_device_ids=true, to_apply=%region_34.35 | all-reduce | flops 1 | bytes 8 | tf_op jit(solution)/shard_map/psum | solution.py:286
  (203 shorter events, 94.5 us)
Async XLA Ops:
  7.2 9.4 copy-start.5
  7.2 81.4 %copy-start.39 = (s32[1024]{0:T(1024)S(1)}, s32[1024]{0:T(1024)}, u32[]{:S(2)}) copy-start(s32[1024]{0:T(1024)} %param.24) | copy-start | bytes 12292
  7.2 81.4 %copy-start.40 = (s32[1024]{0:T(1024)S(1)}, s32[1024]{0:T(1024)}, u32[]{:S(2)}) copy-start(s32[1024]{0:T(1024)} %param.23) | copy-start | bytes 12292
  7.2 82.8 %all-gather.8.cloned.1.call-start = ((), (), s32[]{:S(2)}) async-start(), calls=%async_computation.5 | async-start | bytes 2162688 | tf_op jit(solution)/shard_map/all_gather | solution.py:42
  9.0 118.5 %all-gather.6.cloned.1.call-start = ((), (), s32[]{:S(2)}) async-start(), calls=%async_computation.4 | async-start | bytes 1081344 | tf_op jit(solution)/shard_map/all_gather | solution.py:43
  10.5 172.3 %all-gather.10.cloned.1.call-start = ((), (), s32[]{:S(2)}) async-start(), calls=%async_computation.6 | async-start | bytes 2162688 | tf_op jit(solution)/shard_map/all_gather | solution.py:44
  12.1 229.0 %all-gather.12.cloned.1.call-start = ((), (), s32[]{:S(2)}) async-start(), calls=%async_computation.7 | async-start | bytes 2162688 | tf_op jit(solution)/shard_map/all_gather | solution.py:45
  13.8 539.9 %reduce-scatter.13.cloned.1.call-start = ((), (), s32[]{:S(2)}) async-start(), calls=%async_computation.11 | async-start | bytes 270336
  88.6 367.8 %copy-start.42 = (f32[1,512]{1,0:T(1,128)}, f32[1,512]{1,0:T(1,128)S(1)}, u32[]{:S(2)}) copy-start(f32[1,512]{1,0:T(1,128)S(1)} %get-tuple-element.153) | copy-start | bytes 6148
  97.6 13.6 %copy-start.19 = (bf16[1,512,512]{1,2,0:T(8,128)(2,1)}, bf16[1,512,512]{1,2,0:T(8,128)(2,1)S(1)}, u32[]{:S(2)}) copy-start(bf16[1,512,512]{1,2,0:T(8,128)(2,1)S(1)} %get-tuple-element.142) | copy-start | bytes 1572868
  97.8 13.4 %copy-start.9 = (bf16[1,1024,512]{1,2,0:T(8,128)(2,1)}, bf16[1,1024,512]{1,2,0:T(8,128)(2,1)S(1)}, u32[]{:S(2)}) copy-start(bf16[1,1024,512]{1,2,0:T(8,128)(2,1)S(1)} %get-tuple-element.144) | copy-start | bytes 3145732
  111.2 13.4 %copy-start.45 = (bf16[8,64,512]{2,1,0:T(8,128)(2,1)}, bf16[8,64,512]{2,1,0:T(8,128)(2,1)S(1)}, u32[]{:S(2)}) copy-start(bf16[8,64,512]{2,1,0:T(8,128)(2,1)S(1)} %fusion.82) | copy-start | bytes 1572868
  241.2 9.7 slice-start.4
  336.2 9.6 copy-start.13
  336.2 17.0 %slice-start = ((s8[16777216]{0:T(1024)(128)(4,1)}), s8[4194304]{0:T(1024)(128)(4,1)S(1)}, s32[]{:S(2)}) async-start(s8[16777216]{0:T(1024)(128)(4,1)} %bitcast.118), calls=%async_computation.13 | async-start | bytes 8388608
  336.2 17.0 %slice-start.1 = ((s8[16777216]{0:T(1024)(128)(4,1)}), s8[4194304]{0:T(1024)(128)(4,1)S(1)}, s32[]{:S(2)}) async-start(s8[16777216]{0:T(1024)(128)(4,1)} %bitcast.118), calls=%async_computation.14 | async-start | bytes 8388608
  336.2 17.0 %slice-start.2 = ((s8[16777216]{0:T(1024)(128)(4,1)}), s8[4194304]{0:T(1024)(128)(4,1)S(1)}, s32[]{:S(2)}) async-start(s8[16777216]{0:T(1024)(128)(4,1)} %bitcast.118), calls=%async_computation.15 | async-start | bytes 8388608
  345.8 7.5 slice-start.3
  345.8 7.5 copy-start.12
  446.2 278.6 %all-reduce.5.cloned.1.call-start = ((), (), s32[]{:S(2)}) async-start(), calls=%async_computation.12 | async-start | bytes 8388608
  456.4 380.8 %reduce-scatter.7.cloned.1.call-start = ((), (), s32[]{:S(2)}) async-start(), calls=%async_computation.8 | async-start | bytes 2162688 | tf_op jit(solution)/shard_map/reduce_scatter | solution.py:279
  461.5 516.3 %reduce-scatter.9.cloned.1.call-start = ((), (), s32[]{:S(2)}) async-start(), calls=%async_computation.9 | async-start | bytes 4325376 | tf_op jit(solution)/shard_map/reduce_scatter | solution.py:280
  468.4 649.9 %reduce-scatter.11.cloned.1.call-start = ((), (), s32[]{:S(2)}) async-start(), calls=%async_computation.10 | async-start | bytes 4325376 | tf_op jit(solution)/shard_map/reduce_scatter | solution.py:281
  478.0 643.9 %copy-start.3 = (f32[1024,512]{1,0:T(8,128)S(1)}, f32[1024,512]{1,0:T(8,128)}, u32[]{:S(2)}) copy-start(f32[1024,512]{1,0:T(8,128)} %get-tuple-element.164) | copy-start | bytes 6291460
  518.1 603.7 %copy-start.41 = (f32[2048]{0:T(1024)}, f32[2048]{0:T(1024)S(1)}, u32[]{:S(2)}) copy-start(f32[2048]{0:T(1024)S(1)} %all-reduce.2) | copy-start | bytes 24580
  1121.9 74.6 %copy-start.30 = (f32[4,16,512]{2,1,0:T(8,128)S(1)}, f32[4,16,512]{2,1,0:T(8,128)}, u32[]{:S(2)}) copy-start(f32[4,16,512]{2,1,0:T(8,128)} %param.26) | copy-start | bytes 393220
  1121.9 78.1 %copy-start.31 = (f32[64,512]{1,0:T(8,128)S(1)}, f32[64,512]{1,0:T(8,128)}, u32[]{:S(2)}) copy-start(f32[64,512]{1,0:T(8,128)} %param.35) | copy-start | bytes 393220
  1121.9 78.1 %copy-start.34 = (f32[64,512]{1,0:T(8,128)S(1)}, f32[64,512]{1,0:T(8,128)}, u32[]{:S(2)}) copy-start(f32[64,512]{1,0:T(8,128)} %reduce-scatter.11.cloned.1.call-done) | copy-start | bytes 393220
  1125.6 76.2 %copy-start.32 = (f32[16,2048]{1,0:T(8,128)S(1)}, f32[16,2048]{1,0:T(8,128)}, u32[]{:S(2)}) copy-start(f32[16,2048]{1,0:T(8,128)} %param.32) | copy-start | bytes 393220
  1125.6 76.2 %copy-start.33 = (f32[16,2048]{1,0:T(8,128)S(1)}, f32[16,2048]{1,0:T(8,128)}, u32[]{:S(2)}) copy-start(f32[16,2048]{1,0:T(8,128)} %reduce-scatter.9.cloned.1.call-done) | copy-start | bytes 393220
  1125.6 76.2 %copy-start.37 = (f32[16,2048]{1,0:T(8,128)S(1)}, f32[16,2048]{1,0:T(8,128)}, u32[]{:S(2)}) copy-start(f32[16,2048]{1,0:T(8,128)} %param.33) | copy-start | bytes 393220
  1125.6 76.2 %copy-start.38 = (f32[16,2048]{1,0:T(8,128)S(1)}, f32[16,2048]{1,0:T(8,128)}, u32[]{:S(2)}) copy-start(f32[16,2048]{1,0:T(8,128)} %param.34) | copy-start | bytes 393220
  (32 other events, 103.2 us)
Sparse Core Ops, SparseCore 0:
  11.5 56.6 all-gather.7
  71.7 52.8 all-gather.5
  128.0 54.7 all-gather.9
  186.1 55.0 all-gather.11
  446.3 107.3 reduce-scatter.12
  559.1 165.6 all-reduce.4
  727.1 109.9 reduce-scatter.6
  839.4 138.3 reduce-scatter.8
  980.0 138.3 reduce-scatter.10
where the time goes:
time: 1210 us
  waiting for transfers between devices  691 us (57%)
  matrix products  237 us (20%)
  blocking collectives  179 us (15%)
  other arithmetic  47.2 us (4%)
  local copies, waits for them, and re-layouts  34.7 us (3%)
  between operations  20.6 us (2%)
    unnamed x11, waiting for transfers between devices  204 us
    reduce_scatter x1, waiting for transfers between devices, body(): lax.psum_scatter(grad_w_out, ('dp', 'inner'), scatter_dimension=0, tiled=...  138 us
    reduce_scatter x1, waiting for transfers between devices, body(): lax.psum_scatter(grad_w_in, ('dp', 'inner'), scatter_dimension=0, tiled=T...  138 us
    reduce_scatter x1, waiting for transfers between devices, body(): lax.psum_scatter(grad_gates, ('dp', 'inner'), scatter_dimension=1, tiled=...  110 us
    unnamed x2, blocking collectives  81.8 us
    psum x1, blocking collectives, body(): grad_norm = jnp.sqrt(lax.psum(local_squares, ('dp', 'inner')))  67.5 us
    dot_general x2, matrix products, attend_back(): jnp.einsum('hqk,khe->qhe', grad_raw, key_heads, preferred_element_type=jn...  66.9 us
    dot_general x2, matrix products, attend_back(): jnp.einsum('hqk,qhe->khe', grad_raw, query_part, preferred_element_type=j...  62.9 us
  transfers between devices with their start and end apart: 9, of which 7 were waited for; matrix products, arithmetic and copies ran while one was open for 8% of the time, Pallas kernels for 0%

commit v1 on v0

--- a/solution.py
+++ b/solution.py
@@ -17,6 +17,29 @@
 masked_score = -1e30
 
 
+def joined_along(blocks, dim):
+    shape = list(blocks.shape[1:])
+    shape[dim] *= blocks.shape[0]
+    return jnp.moveaxis(blocks, 0, dim).reshape(shape)
+
+
+def collected_by_bits(shard, axis):
+    size, place = (lax.axis_size(axis), lax.axis_index(axis))
+    blocks, distance = (shard[None], 1)
+    while distance < size:
+        partner_block = lax.ppermute(blocks, axis, [(i, i ^ distance) for i in range(size)])
+        low = place & distance == 0
+        blocks = jnp.concatenate(
+            [jnp.where(low, blocks, partner_block), jnp.where(low, partner_block, blocks)]
+        )
+        distance *= 2
+    return blocks
+
+
+def collect(x, axis, dim):
+    return joined_along(collected_by_bits(x, axis), dim)
+
+
 def normalize_parts(values, gain_row, bias_row):
     centred = values - jnp.mean(values, -1, keepdims=True)
     spread = jnp.mean(centred * centred, -1, keepdims=True)
@@ -41,7 +64,7 @@
     return (
         lax.all_gather(low_attn, ("dp", "inner"), axis=1, tiled=True),
         lax.all_gather(low_gate, ("dp", "inner"), axis=1, tiled=True),
-        lax.all_gather(low_in, ("dp", "inner"), axis=0, tiled=True),
+        collect(low_in, ("dp", "inner"), 0),
         lax.all_gather(low_out, ("dp", "inner"), axis=0, tiled=True),
         lax.all_gather(low_vec, ("dp", "inner"), axis=1, tiled=True),
         lax.all_gather(low_shift, ("dp", "inner"), axis=0, tiled=True),

time: 1210 us -> 1180 us (0.975)
  waiting for transfers between devices: 691 us -> 612 us
  blocking collectives: 179 us -> 214 us
    all_gather x1 -> x0, waiting for transfers between devices: 49.7 us -> none  [fetch(): lax.all_gather(low_in, ('dp', 'inner'), axis=0, tiled=True)]
    all_gather x1, waiting for transfers between devices: 51.2 us -> 9.9 us  [fetch(): lax.all_gather(low_out, ('dp', 'inner'), axis=0, tiled=True)]
    unnamed x2, blocking collectives: 81.8 us -> 109 us
    unnamed x11 -> x10, waiting for transfers between devices: 204 us -> 204 us
  transfers between devices with their start and end apart: 9 -> 13, of which waited for: 7 -> 9; matrix products, arithmetic and copies ran while one was open for 8% -> 8% of each run, Pallas kernels for 0% -> 0%
where the time goes in v1:
time: 1180 us
  waiting for transfers between devices  612 us (52%)
  matrix products  235 us (20%)
  blocking collectives  214 us (18%)
  other arithmetic  48.5 us (4%)
  local copies, waits for them, and re-layouts  36.3 us (3%)
  between operations  21 us (2%)
    unnamed x10, waiting for transfers between devices  204 us
    reduce_scatter x1, waiting for transfers between devices, body(): lax.psum_scatter(grad_w_out, ('dp', 'inner'), scatter_dimension=0, tiled=...  139 us
    reduce_scatter x1, waiting for transfers between devices, body(): lax.psum_scatter(grad_w_in, ('dp', 'inner'), scatter_dimension=0, tiled=T...  138 us
    reduce_scatter x1, waiting for transfers between devices, body(): lax.psum_scatter(grad_gates, ('dp', 'inner'), scatter_dimension=1, tiled=...  110 us
    unnamed x2, blocking collectives  109 us
    psum x1, blocking collectives, body(): grad_norm = jnp.sqrt(lax.psum(local_squares, ('dp', 'inner')))  67.5 us
    dot_general x2, matrix products, attend_back(): jnp.einsum('hqk,khe->qhe', grad_raw, key_heads, preferred_element_type=jn...  67.1 us
    dot_general x2, matrix products, attend_back(): jnp.einsum('hqk,qhe->khe', grad_raw, query_part, preferred_element_type=j...  62.9 us
  transfers between devices with their start and end apart: 13, of which 9 were waited for; matrix products, arithmetic and copies ran while one was open for 8% of the time, Pallas kernels for 0%

profile of v1, /device:TPU:12, one launch (start us, length us, event | category | flops | bytes accessed | tf_op | source)
XLA Modules:
  0.0 1175.3 jit_solution(3108032962207816453)
XLA Ops:
  20.2 7.2 collective-permute-done.2
  28.0 37.6 %all-gather = bf16[32,16,7]{1,2,0:T(8,128)(2,1)S(1)} all-gather(bf16[1,16,7]{1,2,0:T(8,128)(2,1)S(1)} %convert_bitcast_fusion.2), channel_id=1, replica_groups=mesh['dp'=8,'inner'=4] {'dp','inner'}, dimensions={0}, use_global_device_ids=true | all-gather | bytes 7392 | tf_op jit(solution)/shard_map/all_gather | solution.py:69
  67.5 6.4 collective-permute-start.4
  74.2 68.6 %all-reduce = bf16[2048]{0:T(1024)(128)(2,1)S(1)} all-reduce(bf16[2048]{0:T(1024)(128)(2,1)S(1)} %dynamic-update-slice), channel_id=1, replica_groups=mesh['dp'=8,'inner'=4] {'dp','inner'}, use_global_device_ids=true, to_apply=%add | all-reduce | flops 2048 | bytes 8192
  161.7 3.8 fusion.85
  168.8 4.1 fusion.8
  175.2 3.8 fusion.86
  181.2 5.2 fusion.135
  187.9 5.7 fusion.146
  193.6 9.9 all-gather.9.cloned.1.call-done
  203.5 6.5 fusion.89
  231.4 8.1 fusion.147
  239.5 29.8 %fusion.82 = bf16[8,64,512]{2,1,0:T(8,128)(2,1)} fusion(bf16[1024,8,64]{0,2,1:T(8,128)(2,1)} %bitcast.129, f32[8,512,1024]{2,1,0:T(8,128)} %fusion.147, f32[8,512,1024]{2,1,0:T(8,128)} %copy-done.1, f32[8,512]{1,0:T(8,128)S(1)} %log_add_fusion.1), kind=kOutput, calls=%fused_computation.103 | convolution fusion | flops 566498304 | bytes 35143680 | tf_op jit(solution)/shard_map/hqk,khe->qhe/dot_general | solution.py:136
  269.3 31.1 %fusion.13 = f32[8,64,1024]{2,1,0:T(8,128)} fusion(bf16[512,8,64]{0,2,1:T(8,128)(2,1)} %bitcast.142, f32[8,512,1024]{2,1,0:T(8,128)} %fusion.147, f32[8,512,1024]{2,1,0:T(8,128)} %copy-done.1, f32[8,512]{1,0:T(8,128)S(1)} %log_add_fusion.1), kind=kOutput, calls=%fused_computation.20 | convolution fusion | flops 566236160 | bytes 36192256 | tf_op jit(solution)/shard_map/hqk,qhe->khe/dot_general | solution.py:140
  300.4 9.5 fusion.148
  310.0 7.4 fusion.24
  317.5 3.8 add_convert_fusion
  325.7 37.3 %fusion.79 = bf16[8,64,512]{2,1,0:T(8,128)(2,1)} fusion(bf16[1024,8,64]{0,2,1:T(8,128)(2,1)S(1)} %bitcast.130, f32[8,512,1024]{2,1,0:T(8,128)} %fusion.148, f32[8,512,1024]{2,1,0:T(8,128)} %copy-done, f32[8,512]{1,0:T(8,128)S(1)} %log_add_fusion), kind=kOutput, calls=%fused_computation.102 | convolution fusion | flops 566498304 | bytes 35143680 | tf_op jit(solution)/shard_map/hqk,khe->qhe/dot_general | solution.py:136
  363.1 31.8 %add_convert_fusion.1 = bf16[8,64,1024]{2,1,0:T(8,128)(2,1)} fusion(f32[8,64,1024]{2,1,0:T(8,128)} %fusion.13, bf16[512,8,64]{0,2,1:T(8,128)(2,1)} %bitcast.140, f32[8,512,1024]{2,1,0:T(8,128)} %fusion.148, f32[8,512,1024]{2,1,0:T(8,128)} %copy-done, f32[8,512]{1,0:T(8,128)S(1)} %log_add_fusion), kind=kOutput, calls=%fused_computation.77 | convolution fusion | flops 567284736 | bytes 37240832 | tf_op jit(solution)/shard_map/hqk,qhe->khe/dot_general | solution.py:140
  403.4 3.7 convolution_bitcast_fusion
  410.6 4.6 pad_maximum_fusion
  415.2 5.4 copy.128
  426.0 6.7 fusion.66
  434.3 8.0 fusion.88
  442.3 40.1 %all-reduce.2 = f32[2048]{0:T(1024)S(1)} all-reduce(f32[2048]{0:T(1024)S(1)} %get-tuple-element.178), channel_id=7, replica_groups=mesh['dp'=8,'inner'=4] {'dp','inner'}, use_global_device_ids=true, to_apply=%region_32.33.clone | all-reduce | flops 2048 | bytes 16384
  483.7 34.3 %reduce-scatter.13.cloned.1.call-done = f32[16,7]{1,0:T(8,128)} async-done(((f32[512,7]{1,0:T(8,128)}), f32[16,7]{1,0:T(8,128)}) %reduce-scatter.13.cloned.1.call-update) | async-done | bytes 464
  519.4 169.8 %all-reduce.5.cloned.1.call-done = f32[4,512,512]{2,0,1:T(4,128)} async-done(((f32[4,512,512]{2,0,1:T(4,128)}), f32[4,512,512]{2,0,1:T(4,128)}) %all-reduce.5.cloned.1.call-update) | async-done | bytes 4194320
  691.3 110.2 %reduce-scatter.7.cloned.1.call-done = f32[2,16,512]{2,1,0:T(8,128)} async-done(((f32[2,512,512]{2,1,0:T(8,128)}), f32[2,16,512]{2,1,0:T(8,128)}) %reduce-scatter.7.cloned.1.call-update) | async-done | bytes 65552 | tf_op jit(solution)/shard_map/reduce_scatter | solution.py:302
  804.3 137.8 %reduce-scatter.9.cloned.1.call-done = f32[16,2048]{1,0:T(8,128)} async-done(((f32[512,2048]{1,0:T(8,128)}), f32[16,2048]{1,0:T(8,128)}) %reduce-scatter.9.cloned.1.call-update) | async-done | bytes 131088 | tf_op jit(solution)/shard_map/reduce_scatter | solution.py:303
  944.3 138.7 %reduce-scatter.11.cloned.1.call-done = f32[64,512]{1,0:T(8,128)} async-done(((f32[2048,512]{1,0:T(8,128)}), f32[64,512]{1,0:T(8,128)}) %reduce-scatter.11.cloned.1.call-update) | async-done | bytes 131088 | tf_op jit(solution)/shard_map/reduce_scatter | solution.py:304
  1086.5 3.7 fusion.56
  1090.2 67.5 %psum.7 = f32[]{:T(128)} all-reduce(f32[]{:T(128)S(6)} %add.302), channel_id=1, replica_groups=mesh['dp'=8,'inner'=4] {'dp','inner'}, use_global_device_ids=true, to_apply=%region_34.35 | all-reduce | flops 1 | bytes 8 | tf_op jit(solution)/shard_map/psum | solution.py:309
  (232 shorter events, 106.4 us)
Async XLA Ops:
  7.2 12.7 %copy-start.5 = (bf16[1024,512]{1,0:T(8,128)(2,1)S(1)}, bf16[1024,512]{1,0:T(8,128)(2,1)}, u32[]{:S(2)}) copy-start(bf16[1024,512]{1,0:T(8,128)(2,1)} %param.22) | copy-start | bytes 3145732
  7.2 139.1 %all-gather.7.cloned.1.call-start = ((), (), s32[]{:S(2)}) async-start(), calls=%async_computation.5 | async-start | bytes 2162688 | tf_op jit(solution)/shard_map/all_gather | solution.py:65
  9.0 172.2 %all-gather.5.cloned.1.call-start = ((), (), s32[]{:S(2)}) async-start(), calls=%async_computation.4 | async-start | bytes 1081344 | tf_op jit(solution)/shard_map/all_gather | solution.py:66
  10.5 193.0 %all-gather.9.cloned.1.call-start = ((), (), s32[]{:S(2)}) async-start(), calls=%async_computation.6 | async-start | bytes 2162688 | tf_op jit(solution)/shard_map/all_gather | solution.py:68
  11.5 1.3 collective-permute-start
  13.7 5.6 collective-permute-start.1
  16.8 501.2 %reduce-scatter.13.cloned.1.call-start = ((), (), s32[]{:S(2)}) async-start(), calls=%async_computation.10 | async-start | bytes 270336
  19.4 8.0 collective-permute-start.2
  27.5 38.9 %collective-permute-start.3 = (bf16[8,16,2048]{2,1,0:T(8,128)(2,1)S(1)}, bf16[8,16,2048]{2,1,0:T(8,128)(2,1)S(1)}, u32[]{:S(2)}, u32[]{:S(2)}) collective-permute-start(bf16[8,16,2048]{2,1,0:T(8,128)(2,1)S(1)} %pad_maximum_fusion.10), channel_id=1, source_target_pairs={{0,8},{1,9},{2,10},{3,11},{4,12},{5,13},{6,14},{7,15},{8,0},{9,1},... | collective-permute-start | bytes 1572872 | tf_op jit(solution)/shard_map/ppermute | solution.py:30
  66.3 76.4 %copy-start.44 = (s32[1024]{0:T(1024)S(1)}, s32[1024]{0:T(1024)}, u32[]{:S(2)}) copy-start(s32[1024]{0:T(1024)} %param.24) | copy-start | bytes 12292
  66.4 76.4 %copy-start.45 = (s32[1024]{0:T(1024)S(1)}, s32[1024]{0:T(1024)}, u32[]{:S(2)}) copy-start(s32[1024]{0:T(1024)} %param.23) | copy-start | bytes 12292
  67.5 77.1 %collective-permute-start.4 = (bf16[16,16,2048]{2,1,0:T(8,128)(2,1)}, bf16[16,16,2048]{2,1,0:T(8,128)(2,1)S(1)}, u32[]{:S(2)}, u32[]{:S(2)}) collective-permute-start(bf16[16,16,2048]{2,1,0:T(8,128)(2,1)} %pad_maximum_fusion.7), channel_id=1, source_target_pairs={{0,16},{1,17},{2,18},{3,19},{4,20},{5,21},{6,22},{7,23},{8,24},{9,... | collective-permute-start | bytes 3145736 | tf_op jit(solution)/shard_map/ppermute | solution.py:30
  142.8 277.9 %copy-start.48 = (f32[1,512]{1,0:T(1,128)}, f32[1,512]{1,0:T(1,128)S(1)}, u32[]{:S(2)}) copy-start(f32[1,512]{1,0:T(1,128)S(1)} %get-tuple-element.163) | copy-start | bytes 6148
  151.3 14.3 %copy-start.23 = (bf16[1,512,512]{1,2,0:T(8,128)(2,1)}, bf16[1,512,512]{1,2,0:T(8,128)(2,1)S(1)}, u32[]{:S(2)}) copy-start(bf16[1,512,512]{1,2,0:T(8,128)(2,1)S(1)} %get-tuple-element.142) | copy-start | bytes 1572868
  151.5 14.1 %copy-start.9 = (bf16[1,1024,512]{1,2,0:T(8,128)(2,1)}, bf16[1,1024,512]{1,2,0:T(8,128)(2,1)S(1)}, u32[]{:S(2)}) copy-start(bf16[1,1024,512]{1,2,0:T(8,128)(2,1)S(1)} %get-tuple-element.144) | copy-start | bytes 3145732
  165.6 13.5 %copy-start.51 = (bf16[8,64,512]{2,1,0:T(8,128)(2,1)}, bf16[8,64,512]{2,1,0:T(8,128)(2,1)S(1)}, u32[]{:S(2)}) copy-start(bf16[8,64,512]{2,1,0:T(8,128)(2,1)S(1)} %fusion.85) | copy-start | bytes 1572868
  300.4 17.0 %slice-start = ((s8[16777216]{0:T(1024)(128)(4,1)}), s8[4194304]{0:T(1024)(128)(4,1)S(1)}, s32[]{:S(2)}) async-start(s8[16777216]{0:T(1024)(128)(4,1)} %bitcast.121), calls=%async_computation.12 | async-start | bytes 8388608
  300.4 17.0 %slice-start.1 = ((s8[16777216]{0:T(1024)(128)(4,1)}), s8[4194304]{0:T(1024)(128)(4,1)S(1)}, s32[]{:S(2)}) async-start(s8[16777216]{0:T(1024)(128)(4,1)} %bitcast.121), calls=%async_computation.13 | async-start | bytes 8388608
  300.4 17.0 %slice-start.2 = ((s8[16777216]{0:T(1024)(128)(4,1)}), s8[4194304]{0:T(1024)(128)(4,1)S(1)}, s32[]{:S(2)}) async-start(s8[16777216]{0:T(1024)(128)(4,1)} %bitcast.121), calls=%async_computation.14 | async-start | bytes 8388608
  410.5 278.6 %all-reduce.5.cloned.1.call-start = ((), (), s32[]{:S(2)}) async-start(), calls=%async_computation.11 | async-start | bytes 8388608
  420.7 380.8 %reduce-scatter.7.cloned.1.call-start = ((), (), s32[]{:S(2)}) async-start(), calls=%async_computation.7 | async-start | bytes 2162688 | tf_op jit(solution)/shard_map/reduce_scatter | solution.py:302
  425.8 516.2 %reduce-scatter.9.cloned.1.call-start = ((), (), s32[]{:S(2)}) async-start(), calls=%async_computation.8 | async-start | bytes 4325376 | tf_op jit(solution)/shard_map/reduce_scatter | solution.py:303
  432.8 650.2 %reduce-scatter.11.cloned.1.call-start = ((), (), s32[]{:S(2)}) async-start(), calls=%async_computation.9 | async-start | bytes 4325376 | tf_op jit(solution)/shard_map/reduce_scatter | solution.py:304
  442.3 644.1 %copy-start.3 = (f32[1024,512]{1,0:T(8,128)S(1)}, f32[1024,512]{1,0:T(8,128)}, u32[]{:S(2)}) copy-start(f32[1024,512]{1,0:T(8,128)} %get-tuple-element.174) | copy-start | bytes 6291460
  482.4 604.0 %copy-start.47 = (f32[2048]{0:T(1024)}, f32[2048]{0:T(1024)S(1)}, u32[]{:S(2)}) copy-start(f32[2048]{0:T(1024)S(1)} %all-reduce.2) | copy-start | bytes 24580
  1086.5 74.6 %copy-start.36 = (f32[4,16,512]{2,1,0:T(8,128)S(1)}, f32[4,16,512]{2,1,0:T(8,128)}, u32[]{:S(2)}) copy-start(f32[4,16,512]{2,1,0:T(8,128)} %param.26) | copy-start | bytes 393220
  1086.5 78.1 %copy-start.37 = (f32[64,512]{1,0:T(8,128)S(1)}, f32[64,512]{1,0:T(8,128)}, u32[]{:S(2)}) copy-start(f32[64,512]{1,0:T(8,128)} %param.35) | copy-start | bytes 393220
  1086.5 78.1 %copy-start.39 = (f32[64,512]{1,0:T(8,128)S(1)}, f32[64,512]{1,0:T(8,128)}, u32[]{:S(2)}) copy-start(f32[64,512]{1,0:T(8,128)} %reduce-scatter.11.cloned.1.call-done) | copy-start | bytes 393220
  1090.2 76.2 %copy-start.27 = (f32[16,2048]{1,0:T(8,128)S(1)}, f32[16,2048]{1,0:T(8,128)}, u32[]{:S(2)}) copy-start(f32[16,2048]{1,0:T(8,128)} %param.32) | copy-start | bytes 393220
  1090.2 76.2 %copy-start.38 = (f32[16,2048]{1,0:T(8,128)S(1)}, f32[16,2048]{1,0:T(8,128)}, u32[]{:S(2)}) copy-start(f32[16,2048]{1,0:T(8,128)} %reduce-scatter.9.cloned.1.call-done) | copy-start | bytes 393220
  1090.2 76.2 %copy-start.42 = (f32[16,2048]{1,0:T(8,128)S(1)}, f32[16,2048]{1,0:T(8,128)}, u32[]{:S(2)}) copy-start(f32[16,2048]{1,0:T(8,128)} %param.33) | copy-start | bytes 393220
  1090.2 76.2 %copy-start.43 = (f32[16,2048]{1,0:T(8,128)S(1)}, f32[16,2048]{1,0:T(8,128)}, u32[]{:S(2)}) copy-start(f32[16,2048]{1,0:T(8,128)} %param.34) | copy-start | bytes 393220
  (42 other events, 170.4 us)
Sparse Core Ops, SparseCore 0:
  11.4 56.6 all-gather.6
  71.6 73.6 all-gather.4
  148.7 54.7 all-gather.8
  410.7 107.3 reduce-scatter.12
  523.4 165.7 all-reduce.4
  691.3 110.1 reduce-scatter.6
  803.8 138.2 reduce-scatter.8
  944.3 138.5 reduce-scatter.10
